TPU v7x, 32 devices: a whole 2x2x4 slice. The times are simulated.
32 devices in a mesh: video: 2 (over y), rows: 4 (over z), cols: 4 (over x, core).
Axes of the slice: x: 2, y: 2, z: 4, core: 2. Of those that a mesh axis runs over, the one named last changes fastest.
Arguments:
- frame_in: bfloat16 [64, 80, 512], P(('video', 'rows'), 'cols'), parts along dimension 0, may hold values from -6 to 6
- norm_gain: float32 [512], replicated, may hold values from 0.5 to 1.5
- w_query: bfloat16 [512, 512], replicated, may hold values from -2 to 2
- w_key: bfloat16 [512, 512], replicated, may hold values from -0.125 to 0.125
- w_value: bfloat16 [512, 512], replicated, may hold values from -0.25 to 0.25
- w_out: bfloat16 [512, 512], replicated, may hold values from -0.25 to 0.25
- conv_gain: float32 [512], replicated, may hold values from 0.5 to 1.5
- conv_cache: bfloat16 [2, 64, 80, 512], P(None, ('video', 'rows'), 'cols'), parts along dimension 1, may hold values from -6 to 6
- w_conv: bfloat16 [3, 3, 3, 512, 256], replicated, may hold values from -0.0546875 to 0.0546875
- conv_bias: float32 [256], replicated, may hold values from -0.5 to 0.5
Outputs:
- hidden: bfloat16 [64, 80, 512], P(('video', 'rows'), 'cols'), parts along dimension 0
- mixed_out: bfloat16 [64, 80, 256], P(('video', 'rows'), 'cols'), parts along dimension 0
There are 2 independent parts, one for each index of `video`. A program takes and returns all parts, laid end to end along the dimension named above; an argument that names none is the same for every part. Nothing has to cross between parts.
All inputs are finite; a program needn't handle non-finite values.
Results may differ from a plain program's by a relative error of at most 0.012.
Values may be sent and summed in bfloat16 or wider, within the bound.
No kernel may reach another device: no remote copies, remote signals or barrier semaphores. Data moves between devices by JAX's collectives and lax.ppermute only.
A program may use at most 128 MiB of HBM per device.

v0:
```python
import math
import jax
import jax.numpy as jnp
from jax import lax
from jax.sharding import PartitionSpec as P


def padded_2(value, sides, width):
    for axis, dim in sides:
        size, length = (lax.axis_size(axis), value.shape[dim])
        up = [(i, (i + 1) % size) for i in range(size - 1)]
        down = [(j, i) for i, j in up]
        last = lax.slice_in_dim(value, length - width, length, axis=dim)
        first = lax.slice_in_dim(value, 0, width, axis=dim)
        before = lax.ppermute(last, axis, up)
        after = lax.ppermute(first, axis, down)
        value = jnp.concatenate([before, value, after], axis=dim)
    return value


def rms_scaled(values, gain):
    mean_sq = jnp.mean(values * values, axis=-1, keepdims=True)
    return values * lax.rsqrt(mean_sq + 1e-06) * gain


def fold_block(running_state, query_keys, block_rows):
    running, total_sum, accumulated = running_state
    scores = lax.dot_general(
        query_keys, block_rows, (((1,), (1,)), ((), ())), preferred_element_type=jnp.float32
    )
    new_max = jnp.maximum(running, jnp.max(scores, axis=1))
    weights = jnp.exp(scores - new_max[:, None])
    total_sum = jnp.sum(weights, axis=1)
    accumulated = jnp.dot(
        weights.astype(jnp.bfloat16), block_rows, preferred_element_type=jnp.float32
    )
    return (new_max, total_sum, accumulated)


def start_for(query_count, channels):
    return (
        jnp.full((query_count,), -1e30, jnp.float32),
        jnp.zeros((query_count,), jnp.float32),
        jnp.zeros((query_count, channels), jnp.float32),
    )


def body(
    frame_in, norm_gain, w_query, w_key, w_value, w_out, conv_gain, conv_cache, w_conv, conv_bias
):
    tile_rows, tile_cols, channels = frame_in.shape
    out_channels = w_conv.shape[4]
    count = tile_rows * tile_cols
    cache_padded = padded_2(conv_cache, (("rows", 1), ("cols", 2)), 1)
    tokens = frame_in.astype(jnp.float32).reshape(count, channels)
    normed = rms_scaled(tokens, norm_gain).astype(jnp.bfloat16)
    query_rows = (
        jnp.dot(normed, w_query, preferred_element_type=jnp.float32) * (1.0 / math.sqrt(channels))
    ).astype(jnp.bfloat16)
    query_keys = jnp.dot(query_rows, w_key.T, preferred_element_type=jnp.float32).astype(
        jnp.bfloat16
    )
    final_state = fold_block(
        start_for(count, channels),
        query_keys,
        lax.all_gather(normed, ("rows", "cols"), axis=0, tiled=True),
    )
    pooled = (final_state[2] / final_state[1][:, None]).astype(jnp.bfloat16)
    attended = jnp.dot(pooled, w_value, preferred_element_type=jnp.float32).astype(jnp.bfloat16)
    hidden = (tokens + jnp.dot(attended, w_out, preferred_element_type=jnp.float32)).astype(
        jnp.bfloat16
    )
    conv_input = jax.nn.silu(rms_scaled(hidden.astype(jnp.float32), conv_gain)).astype(jnp.bfloat16)
    conv_input = conv_input.reshape(1, tile_rows, tile_cols, channels)
    frame_padded = padded_2(conv_input, (("rows", 1), ("cols", 2)), 1)
    padded = jnp.concatenate([cache_padded, frame_padded], axis=0)
    windows = [
        padded[time_off, row_off : row_off + tile_rows, col_off : col_off + tile_cols, :]
        for time_off in range(3)
        for row_off in range(3)
        for col_off in range(3)
    ]
    patches = jnp.concatenate(windows, axis=-1).reshape(count, 27 * channels)
    kernel_rows = w_conv.reshape(27 * channels, out_channels)
    result_sum = hidden[:, :out_channels].astype(jnp.float32) + conv_bias
    result_sum = result_sum + jnp.dot(patches, kernel_rows, preferred_element_type=jnp.float32)
    hidden_out = hidden.reshape(tile_rows, tile_cols, channels)
    mixed_out = result_sum.astype(jnp.bfloat16).reshape(tile_rows, tile_cols, out_channels)
    return (hidden_out, mixed_out)


def solution(mesh):
    in_specs = (
        P(("video", "rows"), "cols", None),
        P(),
        P(),
        P(),
        P(),
        P(),
        P(),
        P(None, ("video", "rows"), "cols", None),
        P(),
        P(),
    )
    out_specs = (P(("video", "rows"), "cols", None), P(("video", "rows"), "cols", None))
    return jax.shard_map(body, mesh=mesh, in_specs=in_specs, out_specs=out_specs, check_vma=False)
```

profile of v0, /device:TPU:0, one launch (start us, length us, event | category | flops | bytes accessed | tf_op | source)
XLA Modules:
  0.0 100.9 jit_solution(12430634139479733988)
XLA Ops:
  7.2 1.1 %copy.97 = f32[8,20,512]{2,1,0:T(8,128)S(1)} copy(bf16[8,20,512]{2,0,1:T(8,128)(2,1)} %param.10) | data formatting | bytes 491520 | tf_op jit(solution)/shard_map/convert_element_type | solution.py:55
  8.3 1.0 %multiply_reduce_fusion = f32[8,20]{0,1:T(8,128)S(1)} fusion(bf16[8,20,512]{2,0,1:T(8,128)(2,1)} %param.10), kind=kLoop, calls=%fused_computation.32 | loop fusion | flops 245600 | bytes 164480 | tf_op jit(solution)/shard_map/reduce_sum | solution.py:22
  9.6 1.5 %multiply_convert_fusion = bf16[160,512]{1,0:T(8,128)(2,1)} fusion(f32[160,512]{1,0:T(8,128)S(1)} %reshape.106, f32[512]{0:T(512)} %param.11, f32[160]{0:T(256)S(1)} %rsqrt.20), kind=kLoop, calls=%fused_computation.31 | loop fusion | flops 245760 | bytes 494208 | tf_op jit(solution)/shard_map/convert_element_type | solution.py:56
  11.0 1.2 %fusion.28 = (bf16[2,1,20,512]{3,1,2,0:T(2,128)(2,1)S(1)}, bf16[2,1,20,512]{3,1,2,0:T(2,128)(2,1)S(1)}) fusion(bf16[2,8,20,512]{3,1,2,0:T(8,128)(2,1)} %param.17), kind=kLoop, calls=%fused_computation.90 | loop fusion | bytes 163840 | tf_op jit(solution)/shard_map/slice | solution.py:13
  12.2 1.3 %collective-permute-start.1 = (bf16[2,1,20,512]{3,1,2,0:T(2,128)(2,1)S(1)}, bf16[2,1,20,512]{3,1,2,0:T(2,128)(2,1)S(1)}, u32[]{:S(2)}, u32[]{:S(2)}) collective-permute-start(bf16[2,1,20,512]{3,1,2,0:T(2,128)(2,1)S(1)} %get-tuple-element.37), channel_id=1, source_target_pairs={{4,0},{8,4},{12,8},{5,1},{9,5},{13,9},{6,2},{10,6},{14,10},{7,3},{... | collective-permute-start | bytes 122888 | tf_op jit(solution)/shard_map/ppermute | solution.py:16
  13.5 5.6 %collective-permute-start = (bf16[2,1,20,512]{3,1,2,0:T(2,128)(2,1)S(1)}, bf16[2,1,20,512]{3,1,2,0:T(2,128)(2,1)S(1)}, u32[]{:S(2)}, u32[]{:S(2)}) collective-permute-start(bf16[2,1,20,512]{3,1,2,0:T(2,128)(2,1)S(1)} %get-tuple-element.36), channel_id=1, source_target_pairs={{0,4},{4,8},{8,12},{1,5},{5,9},{9,13},{2,6},{6,10},{10,14},{3,7},{... | collective-permute-start | bytes 122888 | tf_op jit(solution)/shard_map/ppermute | solution.py:15
  19.1 1.4 %fusion.2 = bf16[160,512]{1,0:T(8,128)(2,1)S(1)} fusion(bf16[160,512]{1,0:T(8,128)(2,1)} %multiply_convert_fusion, bf16[512,512]{1,0:T(8,128)(2,1)} %param.12), kind=kOutput, calls=%fused_computation.6 | convolution fusion | flops 84049920 | bytes 851968 | tf_op jit(solution)/shard_map/dot_general | solution.py:58
  20.5 1.0 %constant_dynamic-update-slice_fusion.1 = bf16[2,9,20,512]{3,1,2,0:T(8,128)(2,1)S(1)} fusion(bf16[2,8,20,512]{3,1,2,0:T(8,128)(2,1)} %param.17), kind=kLoop, calls=%fused_computation.49 | loop fusion | bytes 655360
  21.6 0.8 pad_maximum_fusion.7
  22.3 1.3 %collective-permute-start.3 = (bf16[2,10,1,512]{3,1,2,0:T(8,128)(2,1)S(1)}, bf16[2,10,1,512]{3,1,2,0:T(8,128)(2,1)S(1)}, u32[]{:S(2)}, u32[]{:S(2)}) collective-permute-start(bf16[2,10,1,512]{3,1,2,0:T(8,128)(2,1)S(1)} %get-tuple-element.28), channel_id=1, source_target_pairs={{1,0},{2,1},{3,2},{5,4},{6,5},{7,6},{9,8},{10,9},{11,10},{13,12},{... | collective-permute-start | bytes 61448 | tf_op jit(solution)/shard_map/ppermute | solution.py:16
  23.6 3.0 %collective-permute-start.2 = (bf16[2,10,1,512]{3,1,2,0:T(8,128)(2,1)S(1)}, bf16[2,10,1,512]{3,1,2,0:T(8,128)(2,1)S(1)}, u32[]{:S(2)}, u32[]{:S(2)}) collective-permute-start(bf16[2,10,1,512]{3,1,2,0:T(8,128)(2,1)S(1)} %get-tuple-element.29), channel_id=1, source_target_pairs={{0,1},{1,2},{2,3},{4,5},{5,6},{6,7},{8,9},{9,10},{10,11},{12,13},{... | collective-permute-start | bytes 61448 | tf_op jit(solution)/shard_map/ppermute | solution.py:15
  26.7 0.1 constant_dynamic-update-slice_fusion
  26.8 0.2 fusion.27
  27.8 0.6 pad_maximum_fusion
  28.4 1.2 %fusion.24 = (bf16[1,8,20,512]{3,1,2,0:T(8,128)(2,1)}, bf16[1,8,20,512]{3,1,2,0:T(8,128)(2,1)S(1)}, bf16[1,8,20,512]{3,1,2,0:T(8,128)(2,1)S(1)}, bf16[1,8,20,512...) fusion(bf16[2,10,21,512]{3,1,2,0:T(8,128)(2,1)S(1)} %get-tuple-, ...), kind=kLoop, calls=%fused_computation.86 | loop fusion | bytes 3932160 | tf_op jit(solution)/shard_map/slice | solution.py:78
  29.7 0.7 concatenate.106
  30.4 1.0 copy.101
  31.4 1.0 copy.102
  32.3 0.7 concatenate.111
  33.0 1.0 copy.104
  34.1 0.7 concatenate.114
  35.3 1.0 copy.114
  36.3 1.6 %constant_dynamic-update-slice_fusion.31 = bf16[160,13824]{1,0:T(8,128)(2,1)} fusion(bf16[160,512]{1,0:T(8,128)(2,1)} %concatenate.106), kind=kLoop, calls=%fused_computation.79 | loop fusion | bytes 327680
  38.0 0.7 constant_dynamic-update-slice_fusion.30
  38.7 0.7 constant_dynamic-update-slice_fusion.29
  39.3 1.6 %constant_dynamic-update-slice_fusion.28 = bf16[160,13824]{1,0:T(8,128)(2,1)} fusion(bf16[160,13824]{1,0:T(8,128)(2,1)} %constant_dynamic-update-slice_fusion.29, bf16[160,512]{1,0:T(8,128)(2,1)} %concatenate.111), kind=kLoop, calls=%fused_computation.76 | loop fusion | bytes 327680
  40.9 0.7 constant_dynamic-update-slice_fusion.27
  41.7 0.7 constant_dynamic-update-slice_fusion.26
  42.4 1.6 %constant_dynamic-update-slice_fusion.25 = bf16[160,13824]{1,0:T(8,128)(2,1)} fusion(bf16[160,13824]{1,0:T(8,128)(2,1)} %constant_dynamic-update-slice_fusion.26, bf16[160,512]{1,0:T(8,128)(2,1)} %concatenate.114), kind=kLoop, calls=%fused_computation.73 | loop fusion | bytes 327680
  43.9 0.7 constant_dynamic-update-slice_fusion.24
  44.7 0.7 constant_dynamic-update-slice_fusion.23
  45.4 0.7 constant_dynamic-update-slice_fusion.22
  46.1 0.7 constant_dynamic-update-slice_fusion.21
  46.8 0.7 constant_dynamic-update-slice_fusion.20
  47.5 0.7 constant_dynamic-update-slice_fusion.19
  48.2 0.7 constant_dynamic-update-slice_fusion.18
  48.9 0.7 constant_dynamic-update-slice_fusion.17
  49.5 0.7 constant_dynamic-update-slice_fusion.16
  50.2 6.4 %all-gather.2.cloned.1.call-done = bf16[2560,512]{1,0:T(8,128)(2,1)} async-done(((bf16[160,512]{1,0:T(8,128)(2,1)}), bf16[2560,512]{1,0:T(8,128)(2,1)}) %all-gather.2.cloned.1.call-update) | async-done | bytes 2621456 | tf_op jit(solution)/shard_map/all_gather | solution.py:66
  56.6 3.1 %fusion.31 = (f32[160]{0:T(256)S(1)}, f32[160,2560]{1,0:T(8,128)S(1)}) fusion(bf16[2560,512]{1,0:T(8,128)(2,1)} %all-gather.2.cloned.1.call-done, bf16[160,512]{1,0:T(8,128)(2,1)S(1)} %fusion.2, bf16[512,512]{1,0:T(8,128)(2,1)S(1)} %copy-done), kind=kOutput, calls=%fused_computation.93 | convolution fusion | flops 503807840 | bytes 4948608 | tf_op jit(solution)/shard_map/dot_general | solution.py:28
  59.8 0.4 fusion
  60.1 3.3 %convolution_convert_fusion = bf16[160,512]{1,0:T(8,128)(2,1)} fusion(bf16[512,512]{1,0:T(8,128)(2,1)} %param.14, bf16[2560,512]{1,0:T(8,128)(2,1)} %all-gather.2.cloned.1.call-done, f32[160,2560]{1,0:T(8,128)S(1)} %get-tuple-element.55, f32[160]{0:T(256)S(1)} %broadcast_maximum_fusion, f32[160]{0:T(256)S(1)} %fusion), kind=kOutput, calls=%fused_computation.8 | convolution fusion | flops 504381440 | bytes 4949248 | tf_op jit(solution)/shard_map/dot_general | solution.py:69
  63.5 1.3 %fusion.11 = (f32[160]{0:T(256)S(1)}, bf16[160,512]{1,0:T(8,128)(2,1)S(1)}) fusion(f32[160,512]{1,0:T(8,128)S(1)} %reshape.106, bf16[160,512]{1,0:T(8,128)(2,1)} %convolution_convert_fusion, bf16[512,512]{1,0:T(8,128)(2,1)S(1)} %copy-done.3), kind=kOutput, calls=%fused_computation.23 | convolution fusion | flops 84295520 | bytes 1180288 | tf_op jit(solution)/shard_map/dot_general | solution.py:70
  64.8 0.2 fusion.18
  65.0 3.1 %collective-permute-start.4 = (bf16[1,1,20,512]{3,2,1,0:T(8,128)(2,1)S(1)}, bf16[1,1,20,512]{3,2,1,0:T(8,128)(2,1)S(1)}, u32[]{:S(2)}, u32[]{:S(2)}) collective-permute-start(bf16[1,1,20,512]{3,2,1,0:T(8,128)(2,1)S(1)} %get-tuple-element.53), channel_id=1, source_target_pairs={{0,4},{4,8},{8,12},{1,5},{5,9},{9,13},{2,6},{6,10},{10,14},{3,7},{... | collective-permute-start | bytes 61448 | tf_op jit(solution)/shard_map/ppermute | solution.py:15
  68.1 0.7 constant_dynamic-update-slice_fusion.15
  69.0 1.3 %collective-permute-start.5 = (bf16[1,1,20,512]{3,2,1,0:T(8,128)(2,1)S(1)}, bf16[1,1,20,512]{3,2,1,0:T(8,128)(2,1)S(1)}, u32[]{:S(2)}, u32[]{:S(2)}) collective-permute-start(bf16[1,1,20,512]{3,2,1,0:T(8,128)(2,1)S(1)} %get-tuple-element.52), channel_id=1, source_target_pairs={{4,0},{8,4},{12,8},{5,1},{9,5},{13,9},{6,2},{10,6},{14,10},{7,3},{... | collective-permute-start | bytes 61448 | tf_op jit(solution)/shard_map/ppermute | solution.py:16
  70.3 4.4 %collective-permute-done.5 = bf16[1,1,20,512]{3,2,1,0:T(8,128)(2,1)S(1)} collective-permute-done((bf16[1,1,20,512]{3,2,1,0:T(8,128)(2,1)S(1)}, bf16[1,1,20,512]{3,2,1,0:T(8,128)(2,1)S(1)}, u32[]{:S(2)}, u32[]{:S(2)}) %collective-permute-start.5) | collective-permute-done | bytes 20512 | tf_op jit(solution)/shard_map/ppermute | solution.py:16
  74.8 1.3 %collective-permute-start.7 = (bf16[1,10,1,512]{3,2,1,0:T(2,128)(2,1)S(1)}, bf16[1,10,1,512]{3,2,1,0:T(2,128)(2,1)S(1)}, u32[]{:S(2)}, u32[]{:S(2)}) collective-permute-start(bf16[1,10,1,512]{3,2,1,0:T(2,128)(2,1)S(1)} %get-tuple-element.47), channel_id=1, source_target_pairs={{1,0},{2,1},{3,2},{5,4},{6,5},{7,6},{9,8},{10,9},{11,10},{13,12},{... | collective-permute-start | bytes 30728 | tf_op jit(solution)/shard_map/ppermute | solution.py:16
  76.1 3.0 %collective-permute-start.6 = (bf16[1,10,1,512]{3,2,1,0:T(2,128)(2,1)S(1)}, bf16[1,10,1,512]{3,2,1,0:T(2,128)(2,1)S(1)}, u32[]{:S(2)}, u32[]{:S(2)}) collective-permute-start(bf16[1,10,1,512]{3,2,1,0:T(2,128)(2,1)S(1)} %get-tuple-element.48), channel_id=1, source_target_pairs={{0,1},{1,2},{2,3},{4,5},{5,6},{6,7},{8,9},{9,10},{10,11},{12,13},{... | collective-permute-start | bytes 30728 | tf_op jit(solution)/shard_map/ppermute | solution.py:15
  79.1 0.7 constant_dynamic-update-slice_fusion.14
  79.9 0.7 copy.117
  80.7 0.3 pad_maximum_fusion.1
  81.1 0.7 constant_dynamic-update-slice_fusion.13
  81.8 0.7 constant_dynamic-update-slice_fusion.12
  82.5 0.7 constant_dynamic-update-slice_fusion.11
  83.2 0.7 constant_dynamic-update-slice_fusion.10
  83.9 0.9 constant_dynamic-update-slice_fusion.9
  84.9 0.7 constant_dynamic-update-slice_fusion.8
  85.6 0.7 constant_dynamic-update-slice_fusion.7
  86.3 0.7 constant_dynamic-update-slice_fusion.6
  87.0 0.7 constant_dynamic-update-slice_fusion.5
  87.7 5.7 %fusion.6 = bf16[160,256]{1,0:T(8,128)(2,1)S(1)} fusion(bf16[160,13824]{1,0:T(8,128)(2,1)} %constant_dynamic-update-slice_fusion.5, bf16[13824,256]{1,0:T(8,128)(2,1)} %bitcast.12, bf16[160,512]{1,0:T(8,128)(2,1)S(1)} %get-tuple-element.57, f32[256]{0:T(256)S(1)} %copy-done.5), kind=kOutput, calls=%fused_computation.13 | convolution fusion | flops 1132625920 | bytes 11666432 | tf_op jit(solution)/shard_map/dot_general | solution.py:86
  93.4 0.7 copy.118
  (73 shorter events, 2.2 us)
Async XLA Ops:
  7.2 49.5 %copy-start = (bf16[512,512]{1,0:T(8,128)(2,1)S(1)}, bf16[512,512]{1,0:T(8,128)(2,1)}, u32[]{:S(2)}) copy-start(bf16[512,512]{1,0:T(8,128)(2,1)} %param.13) | copy-start | bytes 1572868
  7.2 19.7 %copy-start.1 = (bf16[2,8,20,512]{3,1,2,0:T(8,128)(2,1)S(1)}, bf16[2,8,20,512]{3,1,2,0:T(8,128)(2,1)}, u32[]{:S(2)}) copy-start(bf16[2,8,20,512]{3,1,2,0:T(8,128)(2,1)} %param.17) | copy-start | bytes 983044
  7.2 49.5 %all-gather.2.cloned.1.call-start = ((), (), s32[]{:S(2)}) async-start(), calls=%async_computation | async-start | bytes 2785280 | tf_op jit(solution)/shard_map/all_gather | solution.py:66
  12.2 9.3 %collective-permute-start.1 = (bf16[2,1,20,512]{3,1,2,0:T(2,128)(2,1)S(1)}, bf16[2,1,20,512]{3,1,2,0:T(2,128)(2,1)S(1)}, u32[]{:S(2)}, u32[]{:S(2)}) collective-permute-start(bf16[2,1,20,512]{3,1,2,0:T(2,128)(2,1)S(1)} %get-tuple-element.37), channel_id=1, source_target_pairs={{4,0},{8,4},{12,8},{5,1},{9,5},{13,9},{6,2},{10,6},{14,10},{7,3},{... | collective-permute-start | bytes 122888 | tf_op jit(solution)/shard_map/ppermute | solution.py:16
  13.5 8.0 %collective-permute-start = (bf16[2,1,20,512]{3,1,2,0:T(2,128)(2,1)S(1)}, bf16[2,1,20,512]{3,1,2,0:T(2,128)(2,1)S(1)}, u32[]{:S(2)}, u32[]{:S(2)}) collective-permute-start(bf16[2,1,20,512]{3,1,2,0:T(2,128)(2,1)S(1)} %get-tuple-element.36), channel_id=1, source_target_pairs={{0,4},{4,8},{8,12},{1,5},{5,9},{9,13},{2,6},{6,10},{10,14},{3,7},{... | collective-permute-start | bytes 122888 | tf_op jit(solution)/shard_map/ppermute | solution.py:15
  22.3 5.4 %collective-permute-start.3 = (bf16[2,10,1,512]{3,1,2,0:T(8,128)(2,1)S(1)}, bf16[2,10,1,512]{3,1,2,0:T(8,128)(2,1)S(1)}, u32[]{:S(2)}, u32[]{:S(2)}) collective-permute-start(bf16[2,10,1,512]{3,1,2,0:T(8,128)(2,1)S(1)} %get-tuple-element.28), channel_id=1, source_target_pairs={{1,0},{2,1},{3,2},{5,4},{6,5},{7,6},{9,8},{10,9},{11,10},{13,12},{... | collective-permute-start | bytes 61448 | tf_op jit(solution)/shard_map/ppermute | solution.py:16
  23.6 4.1 %collective-permute-start.2 = (bf16[2,10,1,512]{3,1,2,0:T(8,128)(2,1)S(1)}, bf16[2,10,1,512]{3,1,2,0:T(8,128)(2,1)S(1)}, u32[]{:S(2)}, u32[]{:S(2)}) collective-permute-start(bf16[2,10,1,512]{3,1,2,0:T(8,128)(2,1)S(1)} %get-tuple-element.29), channel_id=1, source_target_pairs={{0,1},{1,2},{2,3},{4,5},{5,6},{6,7},{8,9},{9,10},{10,11},{12,13},{... | collective-permute-start | bytes 61448 | tf_op jit(solution)/shard_map/ppermute | solution.py:15
  59.7 3.8 %copy-start.3 = (bf16[512,512]{1,0:T(8,128)(2,1)S(1)}, bf16[512,512]{1,0:T(8,128)(2,1)}, u32[]{:S(2)}) copy-start(bf16[512,512]{1,0:T(8,128)(2,1)} %param.15) | copy-start | bytes 1572868
  59.7 5.0 %copy-start.4 = (f32[512]{0:T(512)S(1)}, f32[512]{0:T(512)}, u32[]{:S(2)}) copy-start(f32[512]{0:T(512)} %param.16) | copy-start | bytes 6148
  59.7 9.1 %copy-start.2 = (bf16[1,8,20,512]{3,1,2,0:T(8,128)(2,1)S(1)}, bf16[1,8,20,512]{3,1,2,0:T(8,128)(2,1)}, u32[]{:S(2)}) copy-start(bf16[1,8,20,512]{3,1,2,0:T(8,128)(2,1)} %get-tuple-element.12) | copy-start | bytes 491524
  65.0 5.3 %collective-permute-start.4 = (bf16[1,1,20,512]{3,2,1,0:T(8,128)(2,1)S(1)}, bf16[1,1,20,512]{3,2,1,0:T(8,128)(2,1)S(1)}, u32[]{:S(2)}, u32[]{:S(2)}) collective-permute-start(bf16[1,1,20,512]{3,2,1,0:T(8,128)(2,1)S(1)} %get-tuple-element.53), channel_id=1, source_target_pairs={{0,4},{4,8},{8,12},{1,5},{5,9},{9,13},{2,6},{6,10},{10,14},{3,7},{... | collective-permute-start | bytes 61448 | tf_op jit(solution)/shard_map/ppermute | solution.py:15
  69.0 5.7 %collective-permute-start.5 = (bf16[1,1,20,512]{3,2,1,0:T(8,128)(2,1)S(1)}, bf16[1,1,20,512]{3,2,1,0:T(8,128)(2,1)S(1)}, u32[]{:S(2)}, u32[]{:S(2)}) collective-permute-start(bf16[1,1,20,512]{3,2,1,0:T(8,128)(2,1)S(1)} %get-tuple-element.52), channel_id=1, source_target_pairs={{4,0},{8,4},{12,8},{5,1},{9,5},{13,9},{6,2},{10,6},{14,10},{7,3},{... | collective-permute-start | bytes 61448 | tf_op jit(solution)/shard_map/ppermute | solution.py:16
  74.7 12.9 %copy-start.5 = (f32[256]{0:T(256)S(1)}, f32[256]{0:T(256)}, u32[]{:S(2)}) copy-start(f32[256]{0:T(256)} %param.19) | copy-start | bytes 3076
  74.8 5.9 %collective-permute-start.7 = (bf16[1,10,1,512]{3,2,1,0:T(2,128)(2,1)S(1)}, bf16[1,10,1,512]{3,2,1,0:T(2,128)(2,1)S(1)}, u32[]{:S(2)}, u32[]{:S(2)}) collective-permute-start(bf16[1,10,1,512]{3,2,1,0:T(2,128)(2,1)S(1)} %get-tuple-element.47), channel_id=1, source_target_pairs={{1,0},{2,1},{3,2},{5,4},{6,5},{7,6},{9,8},{10,9},{11,10},{13,12},{... | collective-permute-start | bytes 30728 | tf_op jit(solution)/shard_map/ppermute | solution.py:16
  76.1 4.6 %collective-permute-start.6 = (bf16[1,10,1,512]{3,2,1,0:T(2,128)(2,1)S(1)}, bf16[1,10,1,512]{3,2,1,0:T(2,128)(2,1)S(1)}, u32[]{:S(2)}, u32[]{:S(2)}) collective-permute-start(bf16[1,10,1,512]{3,2,1,0:T(2,128)(2,1)S(1)} %get-tuple-element.48), channel_id=1, source_target_pairs={{0,1},{1,2},{2,3},{4,5},{5,6},{6,7},{8,9},{9,10},{10,11},{12,13},{... | collective-permute-start | bytes 30728 | tf_op jit(solution)/shard_map/ppermute | solution.py:15
Sparse Core Ops, SparseCore 0:
  11.1 45.4 all-gather.1
where the time goes:
time: 102 us; the launch traced here: 101 us
  local copies, waits for them, and re-layouts  34.8 us (34%)
  starting transfers between devices  20 us (20%)
  matrix products  14.7 us (14%)
  between operations  14.7 us (14%)
  waiting for transfers between devices  10.8 us (11%)
  other arithmetic  5.83 us (6%)
    unnamed x41, local copies, waits for them, and re-layouts  22.5 us
    ppermute x4, starting transfers between devices, padded_2(): before = lax.ppermute(last, axis, up)  14.8 us
    all_gather x1, waiting for transfers between devices, body(): lax.all_gather(normed, ('rows', 'cols'), axis=0, tiled=True)  6.41 us
    slice x20, local copies, waits for them, and re-layouts, body(): padded[time_off, row_off:row_off + tile_rows, col_off:col_off + tile_cols...  5.93 us
    dot_general x1, matrix products, body(): jnp.dot(patches, kernel_rows, preferred_element_type=jnp.float32)  5.69 us
    ppermute x4, starting transfers between devices, padded_2(): after = lax.ppermute(first, axis, down)  5.17 us
    ppermute x4, waiting for transfers between devices, padded_2(): after = lax.ppermute(first, axis, down)  4.41 us
    concatenate x27, local copies, waits for them, and re-layouts, body(): patches = jnp.concatenate(windows, axis=-1).reshape(count, 27 * channels)  3.61 us
  transfers between devices with their start and end apart: 9, of which 2 were waited for; matrix products, arithmetic and copies ran while one was open for 30% of the time, Pallas kernels for 0%

commit v1 on v0

--- a/solution.py
+++ b/solution.py
@@ -3,6 +3,18 @@
 import jax.numpy as jnp
 from jax import lax
 from jax.sharding import PartitionSpec as P
+
+
+def doubled_up(value, axis, dim):
+    ways, here = (lax.axis_size(axis), lax.axis_index(axis))
+    grown, reach = (value, 1)
+    while reach < ways:
+        theirs = lax.ppermute(grown, axis, [(d, d ^ reach) for d in range(ways)])
+        mine_first = jnp.concatenate([grown, theirs], axis=dim)
+        theirs_first = jnp.concatenate([theirs, grown], axis=dim)
+        grown = jnp.where(here & reach == 0, mine_first, theirs_first)
+        reach = 2 * reach
+    return grown
 
 
 def padded_2(value, sides, width):
@@ -61,9 +73,7 @@
         jnp.bfloat16
     )
     final_state = fold_block(
-        start_for(count, channels),
-        query_keys,
-        lax.all_gather(normed, ("rows", "cols"), axis=0, tiled=True),
+        start_for(count, channels), query_keys, doubled_up(normed, ("rows", "cols"), 0)
     )
     pooled = (final_state[2] / final_state[1][:, None]).astype(jnp.bfloat16)
     attended = jnp.dot(pooled, w_value, preferred_element_type=jnp.float32).astype(jnp.bfloat16)

time: 102 us -> 149 us (1.46)
  waiting for transfers between devices: 10.8 us -> 51 us
  between operations: 14.7 us -> 1.26 us
  local copies, waits for them, and re-layouts: 34.8 us -> 44.9 us
  starting transfers between devices: 20 us -> 26.5 us
  other arithmetic: 5.83 us -> 8.83 us
    ppermute x0 -> x4, waiting for transfers between devices: none -> 46.5 us  [doubled_up(): theirs = lax.ppermute(grown, axis, [(d, d ^ reach) for d in range(ways)])]
    ppermute x0 -> x4, starting transfers between devices: none -> 7.83 us  [doubled_up(): theirs = lax.ppermute(grown, axis, [(d, d ^ reach) for d in range(ways)])]
    all_gather x1 -> x0, waiting for transfers between devices: 6.41 us -> none  [body(): lax.all_gather(normed, ('rows', 'cols'), axis=0, tiled=True)]
    slice x20, local copies, waits for them, and re-layouts: 5.93 us -> 9.71 us  [body(): padded[time_off, row_off:row_off + tile_rows, col_off:col_off + tile_cols...]
    unnamed x41 -> x43, local copies, waits for them, and re-layouts: 22.5 us -> 26.2 us
    select_n x0 -> x3, other arithmetic: none -> 3.07 us  [doubled_up(): grown = jnp.where(here & reach == 0, mine_first, theirs_first)]
    concatenate x27, local copies, waits for them, and re-layouts: 3.61 us -> 6.3 us  [body(): patches = jnp.concatenate(windows, axis=-1).reshape(count, 27 * channels)]
  transfers between devices with their start and end apart: 9 -> 12, of which waited for: 2 -> 4; matrix products, arithmetic and copies ran while one was open for 30% -> 28% of each run, Pallas kernels for 0% -> 0%
where the time goes in v1:
time: 149 us; the launch traced here: 148 us
  waiting for transfers between devices  51 us (34%)
  local copies, waits for them, and re-layouts  44.9 us (30%)
  starting transfers between devices  26.5 us (18%)
  matrix products  15.9 us (11%)
  other arithmetic  8.83 us (6%)
    ppermute x4, waiting for transfers between devices, doubled_up(): theirs = lax.ppermute(grown, axis, [(d, d ^ reach) for d in range(ways)])  46.5 us
    unnamed x43, local copies, waits for them, and re-layouts  26.2 us
    ppermute x4, starting transfers between devices, padded_2(): before = lax.ppermute(last, axis, up)  13.5 us
    slice x20, local copies, waits for them, and re-layouts, body(): padded[time_off, row_off:row_off + tile_rows, col_off:col_off + tile_cols...  9.71 us
    ppermute x4, starting transfers between devices, doubled_up(): theirs = lax.ppermute(grown, axis, [(d, d ^ reach) for d in range(ways)])  7.83 us
    concatenate x27, local copies, waits for them, and re-layouts, body(): patches = jnp.concatenate(windows, axis=-1).reshape(count, 27 * channels)  6.3 us
    dot_general x1, matrix products, body(): jnp.dot(patches, kernel_rows, preferred_element_type=jnp.float32)  5.69 us
    ppermute x4, starting transfers between devices, padded_2(): after = lax.ppermute(first, axis, down)  5.16 us
  transfers between devices with their start and end apart: 12, of which 4 were waited for; matrix products, arithmetic and copies ran while one was open for 28% of the time, Pallas kernels for 0%

profile of v1, /device:TPU:0, one launch (start us, length us, event | category | flops | bytes accessed | tf_op | source)
XLA Modules:
  0.0 148.4 jit_solution(15365356272997957105)
XLA Ops:
  0.7 1.0 copy.97
  1.7 1.0 multiply_reduce_fusion
  3.0 0.8 multiply_convert_fusion
  4.3 1.2 fusion.31
  5.5 1.3 collective-permute-start.5
  6.8 5.1 %collective-permute-start.4 = (bf16[2,1,20,512]{3,1,2,0:T(2,128)(2,1)S(1)}, bf16[2,1,20,512]{3,1,2,0:T(2,128)(2,1)S(1)}, u32[]{:S(2)}, u32[]{:S(2)}) collective-permute-start(bf16[2,1,20,512]{3,1,2,0:T(2,128)(2,1)S(1)} %get-tuple-element.36), channel_id=1, source_target_pairs={{0,4},{4,8},{8,12},{1,5},{5,9},{9,13},{2,6},{6,10},{10,14},{3,7},{... | collective-permute-start | bytes 122888 | tf_op jit(solution)/shard_map/ppermute | solution.py:27
  11.9 2.0 %fusion.2 = bf16[160,512]{1,0:T(8,128)(2,1)} fusion(bf16[160,512]{1,0:T(8,128)(2,1)S(1)} %multiply_convert_fusion, bf16[512,512]{1,0:T(8,128)(2,1)} %param.12), kind=kOutput, calls=%fused_computation.8 | convolution fusion | flops 84049920 | bytes 851968 | tf_op jit(solution)/shard_map/dot_general | solution.py:70
  13.9 1.0 constant_dynamic-update-slice_fusion.1
  14.9 1.4 pad_maximum_fusion.7
  16.3 1.3 collective-permute-start.7
  17.6 3.0 %collective-permute-start.6 = (bf16[2,10,1,512]{3,1,2,0:T(8,128)(2,1)S(1)}, bf16[2,10,1,512]{3,1,2,0:T(8,128)(2,1)S(1)}, u32[]{:S(2)}, u32[]{:S(2)}) collective-permute-start(bf16[2,10,1,512]{3,1,2,0:T(8,128)(2,1)S(1)} %get-tuple-element.29), channel_id=1, source_target_pairs={{0,1},{1,2},{2,3},{4,5},{5,6},{6,7},{8,9},{9,10},{10,11},{12,13},{... | collective-permute-start | bytes 61448 | tf_op jit(solution)/shard_map/ppermute | solution.py:27
  21.1 2.0 %collective-permute-start.1 = (bf16[320,512]{1,0:T(8,128)(2,1)S(1)}, bf16[320,512]{1,0:T(8,128)(2,1)}, u32[]{:S(2)}, u32[]{:S(2)}) collective-permute-start(bf16[320,512]{1,0:T(8,128)(2,1)S(1)} %maximum_select_fusion.6), channel_id=1, source_target_pairs={{0,2},{1,3},{2,0},{3,1},{4,6},{5,7},{6,4},{7,5},{8,10},{9,11},{10,... | collective-permute-start | bytes 983048 | tf_op jit(solution)/shard_map/ppermute | solution.py:12
  23.4 0.7 concatenate.144
  25.1 6.1 %collective-permute-done.1 = bf16[320,512]{1,0:T(8,128)(2,1)} collective-permute-done((bf16[320,512]{1,0:T(8,128)(2,1)S(1)}, bf16[320,512]{1,0:T(8,128)(2,1)}, u32[]{:S(2)}, u32[]{:S(2)}) %collective-permute-start.1) | collective-permute-done | bytes 327712 | tf_op jit(solution)/shard_map/ppermute | solution.py:12
  31.3 1.3 maximum_select_fusion.2
  32.5 2.5 %collective-permute-start.2 = (bf16[640,512]{1,0:T(8,128)(2,1)S(1)}, bf16[640,512]{1,0:T(8,128)(2,1)}, u32[]{:S(2)}, u32[]{:S(2)}) collective-permute-start(bf16[640,512]{1,0:T(8,128)(2,1)S(1)} %maximum_select_fusion.2), channel_id=1, source_target_pairs={{0,4},{1,5},{2,6},{3,7},{4,0},{5,1},{6,2},{7,3},{8,12},{9,13},{10,... | collective-permute-start | bytes 1966088 | tf_op jit(solution)/shard_map/ppermute | solution.py:12
  35.0 1.3 fusion.27
  36.6 0.7 constant_dynamic-update-slice_fusion.31
  37.4 0.7 constant_dynamic-update-slice_fusion.30
  38.7 0.7 constant_dynamic-update-slice_fusion.28
  39.5 10.6 %collective-permute-done.2 = bf16[640,512]{1,0:T(8,128)(2,1)} collective-permute-done((bf16[640,512]{1,0:T(8,128)(2,1)S(1)}, bf16[640,512]{1,0:T(8,128)(2,1)}, u32[]{:S(2)}, u32[]{:S(2)}) %collective-permute-start.2) | collective-permute-done | bytes 655392 | tf_op jit(solution)/shard_map/ppermute | solution.py:12
  50.1 1.7 %maximum_select_fusion.1 = bf16[1280,512]{1,0:T(8,128)(2,1)S(1)} fusion(bf16[640,512]{1,0:T(8,128)(2,1)} %collective-permute-done.2, bf16[640,512]{1,0:T(8,128)(2,1)S(1)} %maximum_select_fusion.2, pred[]{:T(512)S(6)} %eq.13), kind=kLoop, calls=%fused_computation.4 | loop fusion | flops 5898240 | bytes 2621441 | tf_op jit(solution)/shard_map/jit(_where)/select_n | solution.py:15
  51.8 2.8 %collective-permute-start.3 = (bf16[1280,512]{1,0:T(8,128)(2,1)S(1)}, bf16[1280,512]{1,0:T(8,128)(2,1)}, u32[]{:S(2)}, u32[]{:S(2)}) collective-permute-start(bf16[1280,512]{1,0:T(8,128)(2,1)S(1)} %maximum_select_fusion.1), channel_id=1, source_target_pairs={{0,8},{1,9},{2,10},{3,11},{4,12},{5,13},{6,14},{7,15},{8,0},{9,1},... | collective-permute-start | bytes 3932168 | tf_op jit(solution)/shard_map/ppermute | solution.py:12
  54.6 1.6 %constant_dynamic-update-slice_fusion.27 = bf16[160,13824]{1,0:T(8,128)(2,1)} fusion(bf16[160,13824]{1,0:T(8,128)(2,1)} %constant_dynamic-update-slice_fusion.28, bf16[160,512]{1,0:T(8,128)(2,1)} %concatenate.144), kind=kLoop, calls=%fused_computation.79 | loop fusion | bytes 327680
  56.3 1.0 copy.104
  57.2 0.7 concatenate.145
  57.9 1.0 copy.105
  58.9 0.7 concatenate.146
  59.6 1.0 copy.107
  60.6 0.7 concatenate.149
  61.3 1.0 copy.108
  62.3 0.7 concatenate.150
  63.0 1.0 copy.110
  64.0 1.0 copy.111
  65.0 0.7 concatenate.153
  65.7 1.0 copy.113
  66.7 1.0 copy.114
  67.6 0.7 concatenate.156
  68.3 1.6 %constant_dynamic-update-slice_fusion.26 = bf16[160,13824]{1,0:T(8,128)(2,1)} fusion(bf16[160,13824]{1,0:T(8,128)(2,1)} %constant_dynamic-update-slice_fusion.27, bf16[160,512]{1,0:T(8,128)(2,1)} %concatenate.145), kind=kLoop, calls=%fused_computation.78 | loop fusion | bytes 327680
  70.0 1.6 %constant_dynamic-update-slice_fusion.25 = bf16[160,13824]{1,0:T(8,128)(2,1)} fusion(bf16[160,13824]{1,0:T(8,128)(2,1)} %constant_dynamic-update-slice_fusion.26, bf16[160,512]{1,0:T(8,128)(2,1)} %concatenate.146), kind=kLoop, calls=%fused_computation.77 | loop fusion | bytes 327680
  72.3 1.6 %constant_dynamic-update-slice_fusion.23 = bf16[160,13824]{1,0:T(8,128)(2,1)} fusion(bf16[160,13824]{1,0:T(8,128)(2,1)} %constant_dynamic-update-slice_fusion.24, bf16[160,512]{1,0:T(8,128)(2,1)} %concatenate.149), kind=kLoop, calls=%fused_computation.75 | loop fusion | bytes 327680
  73.9 1.6 %constant_dynamic-update-slice_fusion.22 = bf16[160,13824]{1,0:T(8,128)(2,1)} fusion(bf16[160,13824]{1,0:T(8,128)(2,1)} %constant_dynamic-update-slice_fusion.23, bf16[160,512]{1,0:T(8,128)(2,1)} %concatenate.150), kind=kLoop, calls=%fused_computation.74 | loop fusion | bytes 327680
  76.1 0.7 constant_dynamic-update-slice_fusion.20
  76.8 1.6 %constant_dynamic-update-slice_fusion.19 = bf16[160,13824]{1,0:T(8,128)(2,1)} fusion(bf16[160,13824]{1,0:T(8,128)(2,1)} %constant_dynamic-update-slice_fusion.20, bf16[160,512]{1,0:T(8,128)(2,1)} %concatenate.153), kind=kLoop, calls=%fused_computation.71 | loop fusion | bytes 327680
  79.1 0.7 constant_dynamic-update-slice_fusion.17
  79.8 1.6 %constant_dynamic-update-slice_fusion.16 = bf16[160,13824]{1,0:T(8,128)(2,1)} fusion(bf16[160,13824]{1,0:T(8,128)(2,1)} %constant_dynamic-update-slice_fusion.17, bf16[160,512]{1,0:T(8,128)(2,1)} %concatenate.156), kind=kLoop, calls=%fused_computation.68 | loop fusion | bytes 327680
  81.4 29.8 %collective-permute-done.3 = bf16[1280,512]{1,0:T(8,128)(2,1)} collective-permute-done((bf16[1280,512]{1,0:T(8,128)(2,1)S(1)}, bf16[1280,512]{1,0:T(8,128)(2,1)}, u32[]{:S(2)}, u32[]{:S(2)}) %collective-permute-start.3) | collective-permute-done | bytes 1310752 | tf_op jit(solution)/shard_map/ppermute | solution.py:12
  111.2 4.0 %fusion.34 = (f32[160]{0:T(256)S(1)}, f32[160,2560]{1,0:T(8,128)S(1)}) fusion(bf16[1280,512]{1,0:T(8,128)(2,1)} %collective-permute-done.3, bf16[1280,512]{1,0:T(8,128)(2,1)} %copy-done.2, pred[]{:T(512)S(6)} %eq.12, bf16[160,512]{1,0:T(8,128)(2,1)} %fusion.2, bf16[512,512]{1,0:T(8,128)(2,1)S(1)} %copy-done), kind=kOutput, calls=%fused_computation.99 | convolution fusion | flops 515604320 | bytes 4948609 | tf_op jit(solution)/shard_map/dot_general | solution.py:40
  115.6 3.9 %convolution_convert_fusion = bf16[160,512]{1,0:T(8,128)(2,1)S(1)} fusion(bf16[512,512]{1,0:T(8,128)(2,1)} %param.14, f32[160,2560]{1,0:T(8,128)S(1)} %get-tuple-element.55, f32[160]{0:T(256)S(1)} %broadcast_maximum_fusion, bf16[1280,512]{1,0:T(8,128)(2,1)} %collective-permute-done.3, bf16[1280,512]{1,0:T(8,128)(2,1)} %copy-done.2, pred[]{:T(512)S(6)} %eq.12, ...), kind=kOutput, calls=%fused_computation.10 | convolution fusion | flops 516177920 | bytes 4949249 | tf_op jit(solution)/shard_map/dot_general | solution.py:79
  120.2 2.4 %collective-permute-start.8 = (bf16[1,1,20,512]{3,2,1,0:T(8,128)(2,1)S(1)}, bf16[1,1,20,512]{3,2,1,0:T(8,128)(2,1)S(1)}, u32[]{:S(2)}, u32[]{:S(2)}) collective-permute-start(bf16[1,1,20,512]{3,2,1,0:T(8,128)(2,1)S(1)} %get-tuple-element.53), channel_id=1, source_target_pairs={{0,4},{4,8},{8,12},{1,5},{5,9},{9,13},{2,6},{6,10},{10,14},{3,7},{... | collective-permute-start | bytes 61448 | tf_op jit(solution)/shard_map/ppermute | solution.py:27
  123.3 1.3 collective-permute-start.9
  124.7 4.4 %collective-permute-done.9 = bf16[1,1,20,512]{3,2,1,0:T(8,128)(2,1)S(1)} collective-permute-done((bf16[1,1,20,512]{3,2,1,0:T(8,128)(2,1)S(1)}, bf16[1,1,20,512]{3,2,1,0:T(8,128)(2,1)S(1)}, u32[]{:S(2)}, u32[]{:S(2)}) %collective-permute-start.9) | collective-permute-done | bytes 20512 | tf_op jit(solution)/shard_map/ppermute | solution.py:28
  129.2 1.3 collective-permute-start.11
  130.5 3.0 %collective-permute-start.10 = (bf16[1,10,1,512]{3,2,1,0:T(2,128)(2,1)S(1)}, bf16[1,10,1,512]{3,2,1,0:T(2,128)(2,1)S(1)}, u32[]{:S(2)}, u32[]{:S(2)}) collective-permute-start(bf16[1,10,1,512]{3,2,1,0:T(2,128)(2,1)S(1)} %get-tuple-element.48), channel_id=1, source_target_pairs={{0,1},{1,2},{2,3},{4,5},{5,6},{6,7},{8,9},{9,10},{10,11},{12,13},{... | collective-permute-start | bytes 30728 | tf_op jit(solution)/shard_map/ppermute | solution.py:27
  134.2 0.7 copy.117
  135.5 0.7 constant_dynamic-update-slice_fusion.13
  136.2 0.7 constant_dynamic-update-slice_fusion.12
  136.9 0.7 constant_dynamic-update-slice_fusion.11
  137.6 0.7 constant_dynamic-update-slice_fusion.10
  138.3 0.8 constant_dynamic-update-slice_fusion.9
  139.3 0.7 constant_dynamic-update-slice_fusion.8
  140.0 0.7 constant_dynamic-update-slice_fusion.7
  141.4 0.7 constant_dynamic-update-slice_fusion.5
  142.1 5.7 %fusion.6 = bf16[160,256]{1,0:T(8,128)(2,1)S(1)} fusion(bf16[160,13824]{1,0:T(8,128)(2,1)} %constant_dynamic-update-slice_fusion.5, bf16[13824,256]{1,0:T(8,128)(2,1)} %bitcast.10, bf16[160,512]{1,0:T(8,128)(2,1)S(1)} %get-tuple-element.57, f32[256]{0:T(256)S(1)} %copy-done.6), kind=kOutput, calls=%fused_computation.15 | convolution fusion | flops 1132625920 | bytes 11666432 | tf_op jit(solution)/shard_map/dot_general | solution.py:96
  (83 shorter events, 10.0 us)
Async XLA Ops:
  0.6 110.6 %copy-start = (bf16[512,512]{1,0:T(8,128)(2,1)S(1)}, bf16[512,512]{1,0:T(8,128)(2,1)}, u32[]{:S(2)}) copy-start(bf16[512,512]{1,0:T(8,128)(2,1)} %param.13) | copy-start | bytes 1572868
  0.6 20.0 %copy-start.1 = (bf16[2,8,20,512]{3,1,2,0:T(8,128)(2,1)S(1)}, bf16[2,8,20,512]{3,1,2,0:T(8,128)(2,1)}, u32[]{:S(2)}) copy-start(bf16[2,8,20,512]{3,1,2,0:T(8,128)(2,1)} %param.17) | copy-start | bytes 983044
  3.7 17.2 %collective-permute-start = (bf16[160,512]{1,0:T(8,128)(2,1)S(1)}, bf16[160,512]{1,0:T(8,128)(2,1)S(1)}, u32[]{:S(2)}, u32[]{:S(2)}) collective-permute-start(bf16[160,512]{1,0:T(8,128)(2,1)S(1)} %multiply_convert_fusion), channel_id=1, source_target_pairs={{0,1},{1,0},{2,3},{3,2},{4,5},{5,4},{6,7},{7,6},{8,9},{9,8},{10,11... | collective-permute-start | bytes 491528 | tf_op jit(solution)/shard_map/ppermute | solution.py:12
  5.5 9.4 %collective-permute-start.5 = (bf16[2,1,20,512]{3,1,2,0:T(2,128)(2,1)S(1)}, bf16[2,1,20,512]{3,1,2,0:T(2,128)(2,1)S(1)}, u32[]{:S(2)}, u32[]{:S(2)}) collective-permute-start(bf16[2,1,20,512]{3,1,2,0:T(2,128)(2,1)S(1)} %get-tuple-element.37), channel_id=1, source_target_pairs={{4,0},{8,4},{12,8},{5,1},{9,5},{13,9},{6,2},{10,6},{14,10},{7,3},{... | collective-permute-start | bytes 122888 | tf_op jit(solution)/shard_map/ppermute | solution.py:28
  6.8 8.1 %collective-permute-start.4 = (bf16[2,1,20,512]{3,1,2,0:T(2,128)(2,1)S(1)}, bf16[2,1,20,512]{3,1,2,0:T(2,128)(2,1)S(1)}, u32[]{:S(2)}, u32[]{:S(2)}) collective-permute-start(bf16[2,1,20,512]{3,1,2,0:T(2,128)(2,1)S(1)} %get-tuple-element.36), channel_id=1, source_target_pairs={{0,4},{4,8},{8,12},{1,5},{5,9},{9,13},{2,6},{6,10},{10,14},{3,7},{... | collective-permute-start | bytes 122888 | tf_op jit(solution)/shard_map/ppermute | solution.py:27
  16.3 8.1 %collective-permute-start.7 = (bf16[2,10,1,512]{3,1,2,0:T(8,128)(2,1)}, bf16[2,10,1,512]{3,1,2,0:T(8,128)(2,1)S(1)}, u32[]{:S(2)}, u32[]{:S(2)}) collective-permute-start(bf16[2,10,1,512]{3,1,2,0:T(8,128)(2,1)} %get-tuple-element.28), channel_id=1, source_target_pairs={{1,0},{2,1},{3,2},{5,4},{6,5},{7,6},{9,8},{10,9},{11,10},{13,12},{... | collective-permute-start | bytes 61448 | tf_op jit(solution)/shard_map/ppermute | solution.py:28
  17.6 6.9 %collective-permute-start.6 = (bf16[2,10,1,512]{3,1,2,0:T(8,128)(2,1)S(1)}, bf16[2,10,1,512]{3,1,2,0:T(8,128)(2,1)S(1)}, u32[]{:S(2)}, u32[]{:S(2)}) collective-permute-start(bf16[2,10,1,512]{3,1,2,0:T(8,128)(2,1)S(1)} %get-tuple-element.29), channel_id=1, source_target_pairs={{0,1},{1,2},{2,3},{4,5},{5,6},{6,7},{8,9},{9,10},{10,11},{12,13},{... | collective-permute-start | bytes 61448 | tf_op jit(solution)/shard_map/ppermute | solution.py:27
  21.1 10.2 %collective-permute-start.1 = (bf16[320,512]{1,0:T(8,128)(2,1)S(1)}, bf16[320,512]{1,0:T(8,128)(2,1)}, u32[]{:S(2)}, u32[]{:S(2)}) collective-permute-start(bf16[320,512]{1,0:T(8,128)(2,1)S(1)} %maximum_select_fusion.6), channel_id=1, source_target_pairs={{0,2},{1,3},{2,0},{3,1},{4,6},{5,7},{6,4},{7,5},{8,10},{9,11},{10,... | collective-permute-start | bytes 983048 | tf_op jit(solution)/shard_map/ppermute | solution.py:12
  32.5 17.6 %collective-permute-start.2 = (bf16[640,512]{1,0:T(8,128)(2,1)S(1)}, bf16[640,512]{1,0:T(8,128)(2,1)}, u32[]{:S(2)}, u32[]{:S(2)}) collective-permute-start(bf16[640,512]{1,0:T(8,128)(2,1)S(1)} %maximum_select_fusion.2), channel_id=1, source_target_pairs={{0,4},{1,5},{2,6},{3,7},{4,0},{5,1},{6,2},{7,3},{8,12},{9,13},{10,... | collective-permute-start | bytes 1966088 | tf_op jit(solution)/shard_map/ppermute | solution.py:12
  51.8 27.3 %copy-start.2 = (bf16[1280,512]{1,0:T(8,128)(2,1)}, bf16[1280,512]{1,0:T(8,128)(2,1)S(1)}, u32[]{:S(2)}) copy-start(bf16[1280,512]{1,0:T(8,128)(2,1)S(1)} %maximum_select_fusion.1) | copy-start | bytes 3932164
  51.8 59.4 %collective-permute-start.3 = (bf16[1280,512]{1,0:T(8,128)(2,1)S(1)}, bf16[1280,512]{1,0:T(8,128)(2,1)}, u32[]{:S(2)}, u32[]{:S(2)}) collective-permute-start(bf16[1280,512]{1,0:T(8,128)(2,1)S(1)} %maximum_select_fusion.1), channel_id=1, source_target_pairs={{0,8},{1,9},{2,10},{3,11},{4,12},{5,13},{6,14},{7,15},{8,0},{9,1},... | collective-permute-start | bytes 3932168 | tf_op jit(solution)/shard_map/ppermute | solution.py:12
  115.6 4.0 %copy-start.4 = (bf16[512,512]{1,0:T(8,128)(2,1)S(1)}, bf16[512,512]{1,0:T(8,128)(2,1)}, u32[]{:S(2)}) copy-start(bf16[512,512]{1,0:T(8,128)(2,1)} %param.15) | copy-start | bytes 1572868
  115.6 4.3 %copy-start.5 = (f32[512]{0:T(512)S(1)}, f32[512]{0:T(512)}, u32[]{:S(2)}) copy-start(f32[512]{0:T(512)} %param.16) | copy-start | bytes 6148
  115.6 7.6 %copy-start.3 = (bf16[1,8,20,512]{3,1,2,0:T(8,128)(2,1)S(1)}, bf16[1,8,20,512]{3,1,2,0:T(8,128)(2,1)}, u32[]{:S(2)}) copy-start(bf16[1,8,20,512]{3,1,2,0:T(8,128)(2,1)} %get-tuple-element.12) | copy-start | bytes 491524
  120.2 4.5 %collective-permute-start.8 = (bf16[1,1,20,512]{3,2,1,0:T(8,128)(2,1)S(1)}, bf16[1,1,20,512]{3,2,1,0:T(8,128)(2,1)S(1)}, u32[]{:S(2)}, u32[]{:S(2)}) collective-permute-start(bf16[1,1,20,512]{3,2,1,0:T(8,128)(2,1)S(1)} %get-tuple-element.53), channel_id=1, source_target_pairs={{0,4},{4,8},{8,12},{1,5},{5,9},{9,13},{2,6},{6,10},{10,14},{3,7},{... | collective-permute-start | bytes 61448 | tf_op jit(solution)/shard_map/ppermute | solution.py:27
  123.3 5.7 %collective-permute-start.9 = (bf16[1,1,20,512]{3,2,1,0:T(8,128)(2,1)S(1)}, bf16[1,1,20,512]{3,2,1,0:T(8,128)(2,1)S(1)}, u32[]{:S(2)}, u32[]{:S(2)}) collective-permute-start(bf16[1,1,20,512]{3,2,1,0:T(8,128)(2,1)S(1)} %get-tuple-element.52), channel_id=1, source_target_pairs={{4,0},{8,4},{12,8},{5,1},{9,5},{13,9},{6,2},{10,6},{14,10},{7,3},{... | collective-permute-start | bytes 61448 | tf_op jit(solution)/shard_map/ppermute | solution.py:28
  129.1 12.9 %copy-start.6 = (f32[256]{0:T(256)S(1)}, f32[256]{0:T(256)}, u32[]{:S(2)}) copy-start(f32[256]{0:T(256)} %param.19) | copy-start | bytes 3076
  129.2 5.9 %collective-permute-start.11 = (bf16[1,10,1,512]{3,2,1,0:T(2,128)(2,1)S(1)}, bf16[1,10,1,512]{3,2,1,0:T(2,128)(2,1)S(1)}, u32[]{:S(2)}, u32[]{:S(2)}) collective-permute-start(bf16[1,10,1,512]{3,2,1,0:T(2,128)(2,1)S(1)} %get-tuple-element.47), channel_id=1, source_target_pairs={{1,0},{2,1},{3,2},{5,4},{6,5},{7,6},{9,8},{10,9},{11,10},{13,12},{... | collective-permute-start | bytes 30728 | tf_op jit(solution)/shard_map/ppermute | solution.py:28
  130.5 4.6 %collective-permute-start.10 = (bf16[1,10,1,512]{3,2,1,0:T(2,128)(2,1)S(1)}, bf16[1,10,1,512]{3,2,1,0:T(2,128)(2,1)S(1)}, u32[]{:S(2)}, u32[]{:S(2)}) collective-permute-start(bf16[1,10,1,512]{3,2,1,0:T(2,128)(2,1)S(1)} %get-tuple-element.48), channel_id=1, source_target_pairs={{0,1},{1,2},{2,3},{4,5},{5,6},{6,7},{8,9},{9,10},{10,11},{12,13},{... | collective-permute-start | bytes 30728 | tf_op jit(solution)/shard_map/ppermute | solution.py:27
